TPU v7x, 512 devices: a whole 4x4x16 slice. The times are simulated.
512 devices in a mesh: ra: 64 (over x_lo, z, core), band: 8 (over x_hi, y).
Axes of the slice: x: 4 (x_hi: 2, x_lo: 2; x = x_hi * 2 + x_lo), y: 4, z: 16, core: 2. Of those that a mesh axis runs over, the one named last changes fastest.
Arguments:
- tiles: bfloat16 [16384, 64, 128], P(('ra', 'band')), may hold values from -6 to 6
- tile_patch: int32 [16384], P(('ra', 'band')), may hold values from 0 to 63, as said below
- tile_offset: int32 [16384], P(('ra', 'band')), may hold values from 0 to 128
- tile_weight: bfloat16 [16384], P(('ra', 'band')), may hold values from 0.25 to 4
- visit_band: int32 [2048], P(('ra', 'band')), may hold values from 0 to 5
- coeff_index: int32 [16384], P(('ra', 'band')), may hold values from 0 to 63
- coeff_table: float32 [64, 21], replicated, may hold values from -1.3 to 1.3
- row_kernels: bfloat16 [21, 21], replicated, may hold values from -1.25 to 1.25
- column_kernels: bfloat16 [21, 21], replicated, may hold values from -1.25 to 1.25
- band_weight: float32 [6], replicated, may hold values from 0.3 to 1.5
Outputs:
- band_coadds: float32 [6, 64, 16384], P(None, 'band', 'ra')
- detection: float32 [64, 16384], P('band', 'ra')
Inputs may be any that keep to these rules, and one draw needn't show every extreme that they name: `tile_patch`: tile j is owned by RA index o = j // 256 and by group g = (j // 32) % 8 of visit owners; its patch lies within 2 patches of o around the cycle of 64 patches. Among the tiles of one device at most 16 fall on one patch, and in every draw, for each group g, one patch receives exactly 16 tiles from each of the 5 devices of group g within reach.
All inputs are finite; a program needn't handle non-finite values.
Results may differ from a plain program's by a relative error of at most 0.005.
Values may be sent and summed in bfloat16 or wider, within the bound.
A program may use at most 64 MiB of HBM per device.

v0:
```python
import jax
import jax.numpy as jnp
from jax import lax
from jax.sharding import PartitionSpec as P

PW = 256
BANDS = 6
REACH = 2


HIGHEST_PRECISION = lax.Precision.HIGHEST


def shifted(block, axis, distance):
    devices = range(lax.axis_size(axis))
    route = [((i - distance) % len(devices), i) for i in devices]
    return lax.ppermute(block, axis, route)


def band_matrices(kernels, extent):
    tap_count = kernels.shape[1]
    tap_of = jnp.arange(extent)[None, :] - jnp.arange(extent)[:, None] + tap_count // 2
    tap_hits = (tap_of[None, :, :] == jnp.arange(tap_count)[:, None, None]).astype(jnp.float32)
    return jnp.einsum(
        "kl,lab->kab", kernels.astype(jnp.float32), tap_hits, precision=HIGHEST_PRECISION
    )


def lookup(table_index, coeff_rows):
    one_hot = (table_index[:, None] == jnp.arange(coeff_rows.shape[0])[None, :]).astype(jnp.float32)
    return jnp.dot(one_hot, coeff_rows, precision=HIGHEST_PRECISION)


def match_block(tiles_in, coeffs, colmats, rowmats):
    column_pass = jnp.einsum(
        "jic,kdc->jkid", tiles_in, colmats, preferred_element_type=jnp.float32
    ).astype(jnp.bfloat16)
    scaled = (coeffs[:, :, None, None] * rowmats[None]).astype(jnp.bfloat16)
    return jnp.einsum(
        "jkab,jkbd->jad", scaled, column_pass, preferred_element_type=jnp.float32
    ).astype(jnp.bfloat16)


def place_block(matched, tile_meta):
    weights = tile_meta[:, 0].astype(jnp.float32)
    offsets = tile_meta[:, 1].astype(jnp.int32)
    bands = tile_meta[:, 2].astype(jnp.int32)
    tile_width = matched.shape[2]
    columns = jnp.arange(PW)
    lands = columns[None, None, :] == offsets[:, None, None] + jnp.arange(tile_width)[None, :, None]
    shifter = jnp.where(lands, weights[:, None, None], 0.0).astype(jnp.bfloat16)
    placed = jnp.einsum("jid,jdq->jiq", matched, shifter, preferred_element_type=jnp.float32)
    one_hot = (bands[:, None] == jnp.arange(BANDS)[None, :]).astype(jnp.float32)
    numerator = jnp.einsum("jb,jiq->biq", one_hot, placed, precision=HIGHEST_PRECISION)
    covered = (columns[None, :] >= offsets[:, None]) & (
        columns[None, :] < offsets[:, None] + tile_width
    )
    weight_sum = jnp.einsum(
        "jb,jq->bq", one_hot, jnp.where(covered, weights[:, None], 0.0), precision=HIGHEST_PRECISION
    )
    return (numerator, weight_sum)


def local(
    tiles,
    tile_patch,
    tile_offset,
    tile_weight,
    visit_band,
    coeff_index,
    coeff_table,
    row_kernels,
    column_kernels,
    band_weight,
):
    tile_count = tiles.shape[0]
    tile_rows = tiles.shape[1]
    tile_width = tiles.shape[2]
    capacity = tile_count // 2
    spread = 2 * REACH + 1
    rowmats = band_matrices(row_kernels, tile_rows)
    colmats = band_matrices(column_kernels, tile_width).astype(jnp.bfloat16)
    tile_band = jnp.repeat(visit_band, tile_count // visit_band.shape[0])
    tile_meta = jnp.stack(
        [
            tile_weight.astype(jnp.float32),
            tile_offset.astype(jnp.float32),
            tile_band.astype(jnp.float32),
            coeff_index.astype(jnp.float32),
        ],
        axis=1,
    ).astype(jnp.bfloat16)
    owner_index = lax.axis_index("ra")
    patch_total = lax.axis_size("ra")
    bucket = (tile_patch - owner_index + REACH) % patch_total
    in_bucket = (bucket[:, None] == jnp.arange(spread)[None, :]).astype(jnp.int32)
    earlier = jnp.cumsum(in_bucket, axis=0) - in_bucket
    slot_rank = jnp.sum(earlier * in_bucket, axis=1)
    selector = (
        (bucket[None, None, :] == jnp.arange(spread)[:, None, None])
        & (slot_rank[None, None, :] == jnp.arange(capacity)[None, :, None])
    ).astype(jnp.bfloat16)
    packed = jnp.einsum(
        "bsj,jhd->bshd", selector, tiles, preferred_element_type=jnp.float32
    ).astype(jnp.bfloat16)
    packed_meta = jnp.einsum(
        "bsj,jm->bsm", selector, tile_meta, preferred_element_type=jnp.float32
    ).astype(jnp.bfloat16)
    arrived = [(packed[REACH], packed_meta[REACH])]
    for distance in list(range(-REACH, 0)) + list(range(1, REACH + 1)):
        arrived.append(
            shifted((packed[distance + REACH], packed_meta[distance + REACH]), "ra", distance)
        )
    slots = jnp.concatenate([piece[0] for piece in arrived], axis=0)
    slot_meta = jnp.concatenate([piece[1] for piece in arrived], axis=0)

    def accumulate(carry, block_in):
        tiles_in, meta_in = block_in
        matched = match_block(
            tiles_in, lookup(meta_in[:, 3].astype(jnp.int32), coeff_table), colmats, rowmats
        )
        add_numerator, add_weight = place_block(matched, meta_in)
        return ((carry[0] + add_numerator, carry[1] + add_weight), None)

    start_state = (
        jnp.zeros((BANDS, tile_rows, PW), jnp.float32),
        jnp.zeros((BANDS, PW), jnp.float32),
    )
    (numerator, weight_sum), unused = lax.scan(
        accumulate,
        start_state,
        (slots.reshape(-1, 8, tile_rows, tile_width), slot_meta.reshape(-1, 8, slot_meta.shape[1])),
    )
    row_share = tile_rows // lax.axis_size("band")
    totals, weight_total = lax.psum((numerator, weight_sum), "band")
    own_rows = lax.dynamic_slice_in_dim(totals, lax.axis_index("band") * row_share, row_share, 1)
    band_coadds = own_rows / jnp.maximum(weight_total, 1.0)[:, None, :]
    detection = jnp.einsum("b,biq->iq", band_weight, band_coadds, precision=HIGHEST_PRECISION)
    return (band_coadds, detection)


def solution(mesh):
    return jax.shard_map(
        local,
        mesh=mesh,
        in_specs=(
            P(("ra", "band"), None, None),
            P(("ra", "band")),
            P(("ra", "band")),
            P(("ra", "band")),
            P(("ra", "band")),
            P(("ra", "band")),
            P(),
            P(),
            P(),
            P(),
        ),
        out_specs=(P(None, "band", "ra"), P("band", "ra")),
        check_vma=False,
    )
```

profile of v0, /device:TPU:24, one launch (start us, length us, event | category | flops | bytes accessed | tf_op | source)
XLA Modules:
  0.0 261.1 jit_solution(991310635738176953)
XLA Ops:
  10.6 12.3 %collective-permute-start = (bf16[16,4]{0,1:T(4,128)(2,1)S(1)}, bf16[16,4]{0,1:T(4,128)(2,1)S(1)}, u32[]{:S(2)}, u32[]{:S(2)}) collective-permute-start(bf16[16,4]{0,1:T(4,128)(2,1)S(1)} %get-tuple-element.117), channel_id=1, source_target_pairs={{16,0},{24,8},{32,16},{40,24},{48,32},{56,40},{64,48},{72,56},{80,... | collective-permute-start | bytes 392 | tf_op jit(solution)/shard_map/ppermute | solution.py:17
  22.9 2.1 collective-permute-start.1
  25.0 1.6 convolution_convert_fusion
  26.6 1.0 slice_bitcast_fusion
  27.5 2.9 %collective-permute-start.4 = (bf16[16,64,128]{2,0,1:T(8,128)(2,1)}, bf16[16,64,128]{2,0,1:T(8,128)(2,1)S(1)}, u32[]{:S(2)}, u32[]{:S(2)}) collective-permute-start(bf16[16,64,128]{2,0,1:T(8,128)(2,1)} %get-tuple-element.113), channel_id=1, source_target_pairs={{16,0},{24,8},{32,16},{40,24},{48,32},{56,40},{64,48},{72,56},{80,... | collective-permute-start | bytes 786440 | tf_op jit(solution)/shard_map/ppermute | solution.py:17
  30.4 2.6 collective-permute-start.5
  33.0 1.9 collective-permute-start.6
  36.6 1.0 copy.20
  37.7 3.0 %collective-permute-start.2 = (bf16[16,4]{0,1:T(4,128)(2,1)S(1)}, bf16[16,4]{0,1:T(4,128)(2,1)S(1)}, u32[]{:S(2)}, u32[]{:S(2)}) collective-permute-start(bf16[16,4]{0,1:T(4,128)(2,1)S(1)} %get-tuple-element.115), channel_id=1, source_target_pairs={{504,0},{0,8},{8,16},{16,24},{24,32},{32,40},{40,48},{48,56},{56,6... | collective-permute-start | bytes 392 | tf_op jit(solution)/shard_map/ppermute | solution.py:17
  40.8 2.9 %collective-permute-start.3 = (bf16[16,4]{0,1:T(4,128)(2,1)S(1)}, bf16[16,4]{0,1:T(4,128)(2,1)S(1)}, u32[]{:S(2)}, u32[]{:S(2)}) collective-permute-start(bf16[16,4]{0,1:T(4,128)(2,1)S(1)} %get-tuple-element.114), channel_id=1, source_target_pairs={{496,0},{504,8},{0,16},{8,24},{16,32},{24,40},{32,48},{40,56},{48,... | collective-permute-start | bytes 392 | tf_op jit(solution)/shard_map/ppermute | solution.py:17
  43.7 1.0 collective-permute-done.2
  44.7 1.9 collective-permute-start.7
  46.6 1.7 collective-permute-done.3
  50.9 4.7 %collective-permute-done.7 = bf16[16,64,128]{2,0,1:T(8,128)(2,1)S(1)} collective-permute-done((bf16[16,64,128]{2,0,1:T(8,128)(2,1)S(1)}, bf16[16,64,128]{2,0,1:T(8,128)(2,1)S(1)}, u32[]{:S(2)}, u32[]{:S(2)}) %collective-permute-start.7) | collective-permute-done | bytes 262176 | tf_op jit(solution)/shard_map/ppermute | solution.py:17
  56.4 102.3 %while.13 = (s32[]{:T(128)}, f32[6,64,256]{2,0,1:T(8,128)}, f32[6,256]{1,0:T(8,128)S(1)}, bf16[10,8,4]{1,2,0:T(4,128)(2,1)S(1)}, f32[64,21]{0,1:T(8,128)S(1)}, /...) while((s32[]{:T(128)}, f32[6,64,256]{2,0,1:T(8,128)}, ...), condition=%wide.region_3.4_spmd.clone, body=%wide.region_2.3_spmd.clone.sunk | while | flops 573926016 | bytes 19803496 | solution.py:129
  56.4 1.0 constant_dynamic-slice_fusion.2
  57.5 0.9 fusion.80
  58.4 1.8 copy.64
  60.5 3.2 %fusion.82 = f32[8,64,256]{2,1,0:T(8,128)} fusion(bf16[8,21,64,128]{3,1,2,0:T(8,128)(2,1)S(1)} %bitcast.113, f32[21,64,64]{2,1,0:T(8,128)} %get-tuple-element.203, f32[8,21]{1,0:T(8,128)S(1)} %fusion.81, f32[8]{0:T(128)S(1)} %get-tuple-element.175, s32[8,128]{1,0:T(8,128)S(1)} %iota_add_fusion.2), kind=kOutput, calls=%fused_computation.10.clone.1 | convolution fusion | flops 211681280 | bytes 3625664 | tf_op jit(solution)/shard_map/while/body/eval_jaxpr/jid,jdq->jiq/dot_general | solution.py:52
  63.7 2.6 convolution_add_fusion.4
  66.5 1.1 constant_dynamic-slice_fusion.2
  67.6 0.9 fusion.80
  68.5 1.8 copy.64
  70.6 3.2 %fusion.82 = f32[8,64,256]{2,1,0:T(8,128)} fusion(bf16[8,21,64,128]{3,1,2,0:T(8,128)(2,1)S(1)} %bitcast.113, f32[21,64,64]{2,1,0:T(8,128)} %get-tuple-element.203, f32[8,21]{1,0:T(8,128)S(1)} %fusion.81, f32[8]{0:T(128)S(1)} %get-tuple-element.175, s32[8,128]{1,0:T(8,128)S(1)} %iota_add_fusion.2), kind=kOutput, calls=%fused_computation.10.clone.1 | convolution fusion | flops 211681280 | bytes 3625664 | tf_op jit(solution)/shard_map/while/body/eval_jaxpr/jid,jdq->jiq/dot_general | solution.py:52
  73.8 2.7 %convolution_add_fusion.4 = f32[6,64,256]{2,0,1:T(8,128)} fusion(f32[8,64,256]{2,1,0:T(8,128)} %fusion.82, f32[6,64,256]{2,0,1:T(8,128)} %get-tuple-element.189, pred[]{:T(512)S(6)} %compare.4, s32[8]{0:T(128)S(1)} %get-tuple-element.177), kind=kOutput, calls=%fused_computation.7.clone.1 | convolution fusion | flops 9633840 | bytes 1310753 | tf_op jit(solution)/shard_map/while/body/eval_jaxpr/jb,jiq->biq/dot_general | solution.py:54
  76.8 1.1 constant_dynamic-slice_fusion.2
  77.8 0.9 fusion.80
  78.7 1.8 copy.64
  80.8 3.2 %fusion.82 = f32[8,64,256]{2,1,0:T(8,128)} fusion(bf16[8,21,64,128]{3,1,2,0:T(8,128)(2,1)S(1)} %bitcast.113, f32[21,64,64]{2,1,0:T(8,128)} %get-tuple-element.203, f32[8,21]{1,0:T(8,128)S(1)} %fusion.81, f32[8]{0:T(128)S(1)} %get-tuple-element.175, s32[8,128]{1,0:T(8,128)S(1)} %iota_add_fusion.2), kind=kOutput, calls=%fused_computation.10.clone.1 | convolution fusion | flops 211681280 | bytes 3625664 | tf_op jit(solution)/shard_map/while/body/eval_jaxpr/jid,jdq->jiq/dot_general | solution.py:52
  84.1 2.7 %convolution_add_fusion.4 = f32[6,64,256]{2,0,1:T(8,128)} fusion(f32[8,64,256]{2,1,0:T(8,128)} %fusion.82, f32[6,64,256]{2,0,1:T(8,128)} %get-tuple-element.189, pred[]{:T(512)S(6)} %compare.4, s32[8]{0:T(128)S(1)} %get-tuple-element.177), kind=kOutput, calls=%fused_computation.7.clone.1 | convolution fusion | flops 9633840 | bytes 1310753 | tf_op jit(solution)/shard_map/while/body/eval_jaxpr/jb,jiq->biq/dot_general | solution.py:54
  87.0 1.1 constant_dynamic-slice_fusion.2
  88.1 0.9 fusion.80
  89.0 1.8 copy.64
  91.1 3.2 %fusion.82 = f32[8,64,256]{2,1,0:T(8,128)} fusion(bf16[8,21,64,128]{3,1,2,0:T(8,128)(2,1)S(1)} %bitcast.113, f32[21,64,64]{2,1,0:T(8,128)} %get-tuple-element.203, f32[8,21]{1,0:T(8,128)S(1)} %fusion.81, f32[8]{0:T(128)S(1)} %get-tuple-element.175, s32[8,128]{1,0:T(8,128)S(1)} %iota_add_fusion.2), kind=kOutput, calls=%fused_computation.10.clone.1 | convolution fusion | flops 211681280 | bytes 3625664 | tf_op jit(solution)/shard_map/while/body/eval_jaxpr/jid,jdq->jiq/dot_general | solution.py:52
  94.3 2.7 %convolution_add_fusion.4 = f32[6,64,256]{2,0,1:T(8,128)} fusion(f32[8,64,256]{2,1,0:T(8,128)} %fusion.82, f32[6,64,256]{2,0,1:T(8,128)} %get-tuple-element.189, pred[]{:T(512)S(6)} %compare.4, s32[8]{0:T(128)S(1)} %get-tuple-element.177), kind=kOutput, calls=%fused_computation.7.clone.1 | convolution fusion | flops 9633840 | bytes 1310753 | tf_op jit(solution)/shard_map/while/body/eval_jaxpr/jb,jiq->biq/dot_general | solution.py:54
  97.3 1.1 constant_dynamic-slice_fusion.2
  98.3 0.9 fusion.80
  99.2 1.8 copy.64
  101.3 3.2 %fusion.82 = f32[8,64,256]{2,1,0:T(8,128)} fusion(bf16[8,21,64,128]{3,1,2,0:T(8,128)(2,1)S(1)} %bitcast.113, f32[21,64,64]{2,1,0:T(8,128)} %get-tuple-element.203, f32[8,21]{1,0:T(8,128)S(1)} %fusion.81, f32[8]{0:T(128)S(1)} %get-tuple-element.175, s32[8,128]{1,0:T(8,128)S(1)} %iota_add_fusion.2), kind=kOutput, calls=%fused_computation.10.clone.1 | convolution fusion | flops 211681280 | bytes 3625664 | tf_op jit(solution)/shard_map/while/body/eval_jaxpr/jid,jdq->jiq/dot_general | solution.py:52
  104.6 2.7 %convolution_add_fusion.4 = f32[6,64,256]{2,0,1:T(8,128)} fusion(f32[8,64,256]{2,1,0:T(8,128)} %fusion.82, f32[6,64,256]{2,0,1:T(8,128)} %get-tuple-element.189, pred[]{:T(512)S(6)} %compare.4, s32[8]{0:T(128)S(1)} %get-tuple-element.177), kind=kOutput, calls=%fused_computation.7.clone.1 | convolution fusion | flops 9633840 | bytes 1310753 | tf_op jit(solution)/shard_map/while/body/eval_jaxpr/jb,jiq->biq/dot_general | solution.py:54
  107.5 1.1 constant_dynamic-slice_fusion.2
  108.6 0.9 fusion.80
  109.5 1.8 copy.64
  111.6 3.2 %fusion.82 = f32[8,64,256]{2,1,0:T(8,128)} fusion(bf16[8,21,64,128]{3,1,2,0:T(8,128)(2,1)S(1)} %bitcast.113, f32[21,64,64]{2,1,0:T(8,128)} %get-tuple-element.203, f32[8,21]{1,0:T(8,128)S(1)} %fusion.81, f32[8]{0:T(128)S(1)} %get-tuple-element.175, s32[8,128]{1,0:T(8,128)S(1)} %iota_add_fusion.2), kind=kOutput, calls=%fused_computation.10.clone.1 | convolution fusion | flops 211681280 | bytes 3625664 | tf_op jit(solution)/shard_map/while/body/eval_jaxpr/jid,jdq->jiq/dot_general | solution.py:52
  114.8 2.7 %convolution_add_fusion.4 = f32[6,64,256]{2,0,1:T(8,128)} fusion(f32[8,64,256]{2,1,0:T(8,128)} %fusion.82, f32[6,64,256]{2,0,1:T(8,128)} %get-tuple-element.189, pred[]{:T(512)S(6)} %compare.4, s32[8]{0:T(128)S(1)} %get-tuple-element.177), kind=kOutput, calls=%fused_computation.7.clone.1 | convolution fusion | flops 9633840 | bytes 1310753 | tf_op jit(solution)/shard_map/while/body/eval_jaxpr/jb,jiq->biq/dot_general | solution.py:54
  117.8 1.1 constant_dynamic-slice_fusion.2
  119.7 1.8 copy.64
  121.8 3.2 %fusion.82 = f32[8,64,256]{2,1,0:T(8,128)} fusion(bf16[8,21,64,128]{3,1,2,0:T(8,128)(2,1)S(1)} %bitcast.113, f32[21,64,64]{2,1,0:T(8,128)} %get-tuple-element.203, f32[8,21]{1,0:T(8,128)S(1)} %fusion.81, f32[8]{0:T(128)S(1)} %get-tuple-element.175, s32[8,128]{1,0:T(8,128)S(1)} %iota_add_fusion.2), kind=kOutput, calls=%fused_computation.10.clone.1 | convolution fusion | flops 211681280 | bytes 3625664 | tf_op jit(solution)/shard_map/while/body/eval_jaxpr/jid,jdq->jiq/dot_general | solution.py:52
  125.1 2.7 %convolution_add_fusion.4 = f32[6,64,256]{2,0,1:T(8,128)} fusion(f32[8,64,256]{2,1,0:T(8,128)} %fusion.82, f32[6,64,256]{2,0,1:T(8,128)} %get-tuple-element.189, pred[]{:T(512)S(6)} %compare.4, s32[8]{0:T(128)S(1)} %get-tuple-element.177), kind=kOutput, calls=%fused_computation.7.clone.1 | convolution fusion | flops 9633840 | bytes 1310753 | tf_op jit(solution)/shard_map/while/body/eval_jaxpr/jb,jiq->biq/dot_general | solution.py:54
  128.0 1.1 constant_dynamic-slice_fusion.2
  130.0 1.8 copy.64
  132.1 3.2 %fusion.82 = f32[8,64,256]{2,1,0:T(8,128)} fusion(bf16[8,21,64,128]{3,1,2,0:T(8,128)(2,1)S(1)} %bitcast.113, f32[21,64,64]{2,1,0:T(8,128)} %get-tuple-element.203, f32[8,21]{1,0:T(8,128)S(1)} %fusion.81, f32[8]{0:T(128)S(1)} %get-tuple-element.175, s32[8,128]{1,0:T(8,128)S(1)} %iota_add_fusion.2), kind=kOutput, calls=%fused_computation.10.clone.1 | convolution fusion | flops 211681280 | bytes 3625664 | tf_op jit(solution)/shard_map/while/body/eval_jaxpr/jid,jdq->jiq/dot_general | solution.py:52
  135.3 2.7 %convolution_add_fusion.4 = f32[6,64,256]{2,0,1:T(8,128)} fusion(f32[8,64,256]{2,1,0:T(8,128)} %fusion.82, f32[6,64,256]{2,0,1:T(8,128)} %get-tuple-element.189, pred[]{:T(512)S(6)} %compare.4, s32[8]{0:T(128)S(1)} %get-tuple-element.177), kind=kOutput, calls=%fused_computation.7.clone.1 | convolution fusion | flops 9633840 | bytes 1310753 | tf_op jit(solution)/shard_map/while/body/eval_jaxpr/jb,jiq->biq/dot_general | solution.py:54
  138.2 1.1 constant_dynamic-slice_fusion.2
  140.2 1.8 copy.64
  142.3 3.2 %fusion.82 = f32[8,64,256]{2,1,0:T(8,128)} fusion(bf16[8,21,64,128]{3,1,2,0:T(8,128)(2,1)S(1)} %bitcast.113, f32[21,64,64]{2,1,0:T(8,128)} %get-tuple-element.203, f32[8,21]{1,0:T(8,128)S(1)} %fusion.81, f32[8]{0:T(128)S(1)} %get-tuple-element.175, s32[8,128]{1,0:T(8,128)S(1)} %iota_add_fusion.2), kind=kOutput, calls=%fused_computation.10.clone.1 | convolution fusion | flops 211681280 | bytes 3625664 | tf_op jit(solution)/shard_map/while/body/eval_jaxpr/jid,jdq->jiq/dot_general | solution.py:52
  145.5 2.7 %convolution_add_fusion.4 = f32[6,64,256]{2,0,1:T(8,128)} fusion(f32[8,64,256]{2,1,0:T(8,128)} %fusion.82, f32[6,64,256]{2,0,1:T(8,128)} %get-tuple-element.189, pred[]{:T(512)S(6)} %compare.4, s32[8]{0:T(128)S(1)} %get-tuple-element.177), kind=kOutput, calls=%fused_computation.7.clone.1 | convolution fusion | flops 9633840 | bytes 1310753 | tf_op jit(solution)/shard_map/while/body/eval_jaxpr/jb,jiq->biq/dot_general | solution.py:54
  148.5 1.1 constant_dynamic-slice_fusion.2
  150.5 1.8 copy.64
  152.6 3.2 %fusion.82 = f32[8,64,256]{2,1,0:T(8,128)} fusion(bf16[8,21,64,128]{3,1,2,0:T(8,128)(2,1)S(1)} %bitcast.113, f32[21,64,64]{2,1,0:T(8,128)} %get-tuple-element.203, f32[8,21]{1,0:T(8,128)S(1)} %fusion.81, f32[8]{0:T(128)S(1)} %get-tuple-element.175, s32[8,128]{1,0:T(8,128)S(1)} %iota_add_fusion.2), kind=kOutput, calls=%fused_computation.10.clone.1 | convolution fusion | flops 211681280 | bytes 3625664 | tf_op jit(solution)/shard_map/while/body/eval_jaxpr/jid,jdq->jiq/dot_general | solution.py:52
  155.8 2.7 %convolution_add_fusion.4 = f32[6,64,256]{2,0,1:T(8,128)} fusion(f32[8,64,256]{2,1,0:T(8,128)} %fusion.82, f32[6,64,256]{2,0,1:T(8,128)} %get-tuple-element.189, pred[]{:T(512)S(6)} %compare.4, s32[8]{0:T(128)S(1)} %get-tuple-element.177), kind=kOutput, calls=%fused_computation.7.clone.1 | convolution fusion | flops 9633840 | bytes 1310753 | tf_op jit(solution)/shard_map/while/body/eval_jaxpr/jb,jiq->biq/dot_general | solution.py:54
  158.8 1.9 copy.23
  160.7 19.1 %psum.15 = f32[6,256]{1,0:T(8,128)S(1)} all-reduce(f32[6,256]{1,0:T(8,128)S(1)} %get-tuple-element.46), channel_id=1, replica_groups=mesh['ra'=64,'band'=8] {'band'}, use_global_device_ids=true, to_apply=%region_5.6 | all-reduce | flops 1536 | bytes 12288 | tf_op jit(solution)/shard_map/psum | solution.py:135
  179.8 72.9 %all-reduce.2.cloned.1.call-done = f32[6,64,256]{2,1,0:T(8,128)} async-done(((f32[6,64,256]{2,1,0:T(8,128)}), f32[6,64,256]{2,1,0:T(8,128)}) %all-reduce.2.cloned.1.call-update) | async-done | bytes 393232 | tf_op jit(solution)/shard_map/psum | solution.py:135
  (152 shorter events, 18.3 us)
Async XLA Ops:
  7.2 27.8 %copy-start = (bf16[21,21]{1,0:T(8,128)(2,1)S(1)}, bf16[21,21]{1,0:T(8,128)(2,1)}, u32[]{:S(2)}) copy-start(bf16[21,21]{1,0:T(8,128)(2,1)} %param.20) | copy-start | bytes 2650
  7.2 245.5 %all-reduce.2.cloned.1.call-start = ((), (), s32[]{:S(2)}) async-start(), calls=%async_computation | async-start | bytes 786432 | tf_op jit(solution)/shard_map/psum | solution.py:135
  10.6 27.1 %collective-permute-start = (bf16[16,4]{0,1:T(4,128)(2,1)S(1)}, bf16[16,4]{0,1:T(4,128)(2,1)S(1)}, u32[]{:S(2)}, u32[]{:S(2)}) collective-permute-start(bf16[16,4]{0,1:T(4,128)(2,1)S(1)} %get-tuple-element.117), channel_id=1, source_target_pairs={{16,0},{24,8},{32,16},{40,24},{48,32},{56,40},{64,48},{72,56},{80,... | collective-permute-start | bytes 392 | tf_op jit(solution)/shard_map/ppermute | solution.py:17
  22.9 17.8 %collective-permute-start.1 = (bf16[16,4]{0,1:T(4,128)(2,1)S(1)}, bf16[16,4]{0,1:T(4,128)(2,1)S(1)}, u32[]{:S(2)}, u32[]{:S(2)}) collective-permute-start(bf16[16,4]{0,1:T(4,128)(2,1)S(1)} %get-tuple-element.116), channel_id=1, source_target_pairs={{8,0},{16,8},{24,16},{32,24},{40,32},{48,40},{56,48},{64,56},{72,6... | collective-permute-start | bytes 392 | tf_op jit(solution)/shard_map/ppermute | solution.py:17
  26.6 8.9 %copy-start.4 = (bf16[21,21]{1,0:T(8,128)(2,1)S(1)}, bf16[21,21]{1,0:T(8,128)(2,1)}, u32[]{:S(2)}) copy-start(bf16[21,21]{1,0:T(8,128)(2,1)} %param.19) | copy-start | bytes 2650
  27.5 21.0 %collective-permute-start.4 = (bf16[16,64,128]{2,0,1:T(8,128)(2,1)}, bf16[16,64,128]{2,0,1:T(8,128)(2,1)S(1)}, u32[]{:S(2)}, u32[]{:S(2)}) collective-permute-start(bf16[16,64,128]{2,0,1:T(8,128)(2,1)} %get-tuple-element.113), channel_id=1, source_target_pairs={{16,0},{24,8},{32,16},{40,24},{48,32},{56,40},{64,48},{72,56},{80,... | collective-permute-start | bytes 786440 | tf_op jit(solution)/shard_map/ppermute | solution.py:17
  30.4 18.9 %collective-permute-start.5 = (bf16[16,64,128]{2,0,1:T(8,128)(2,1)}, bf16[16,64,128]{2,0,1:T(8,128)(2,1)S(1)}, u32[]{:S(2)}, u32[]{:S(2)}) collective-permute-start(bf16[16,64,128]{2,0,1:T(8,128)(2,1)} %get-tuple-element.112), channel_id=1, source_target_pairs={{8,0},{16,8},{24,16},{32,24},{40,32},{48,40},{56,48},{64,56},{72,6... | collective-permute-start | bytes 786440 | tf_op jit(solution)/shard_map/ppermute | solution.py:17
  33.0 17.1 %collective-permute-start.6 = (bf16[16,64,128]{2,0,1:T(8,128)(2,1)}, bf16[16,64,128]{2,0,1:T(8,128)(2,1)S(1)}, u32[]{:S(2)}, u32[]{:S(2)}) collective-permute-start(bf16[16,64,128]{2,0,1:T(8,128)(2,1)} %get-tuple-element.111), channel_id=1, source_target_pairs={{504,0},{0,8},{8,16},{16,24},{24,32},{32,40},{40,48},{48,56},{56,6... | collective-permute-start | bytes 786440 | tf_op jit(solution)/shard_map/ppermute | solution.py:17
  37.7 18.8 %copy-start.6 = (f32[64,21]{0,1:T(8,128)S(1)}, f32[64,21]{0,1:T(8,128)}, u32[]{:S(2)}) copy-start(f32[64,21]{0,1:T(8,128)} %param.18) | copy-start | bytes 16132
  37.7 7.0 %collective-permute-start.2 = (bf16[16,4]{0,1:T(4,128)(2,1)S(1)}, bf16[16,4]{0,1:T(4,128)(2,1)S(1)}, u32[]{:S(2)}, u32[]{:S(2)}) collective-permute-start(bf16[16,4]{0,1:T(4,128)(2,1)S(1)} %get-tuple-element.115), channel_id=1, source_target_pairs={{504,0},{0,8},{8,16},{16,24},{24,32},{32,40},{40,48},{48,56},{56,6... | collective-permute-start | bytes 392 | tf_op jit(solution)/shard_map/ppermute | solution.py:17
  40.8 7.6 %collective-permute-start.3 = (bf16[16,4]{0,1:T(4,128)(2,1)S(1)}, bf16[16,4]{0,1:T(4,128)(2,1)S(1)}, u32[]{:S(2)}, u32[]{:S(2)}) collective-permute-start(bf16[16,4]{0,1:T(4,128)(2,1)S(1)} %get-tuple-element.114), channel_id=1, source_target_pairs={{496,0},{504,8},{0,16},{8,24},{16,32},{24,40},{32,48},{40,56},{48,... | collective-permute-start | bytes 392 | tf_op jit(solution)/shard_map/ppermute | solution.py:17
  44.7 10.9 %collective-permute-start.7 = (bf16[16,64,128]{2,0,1:T(8,128)(2,1)S(1)}, bf16[16,64,128]{2,0,1:T(8,128)(2,1)S(1)}, u32[]{:S(2)}, u32[]{:S(2)}) collective-permute-start(bf16[16,64,128]{2,0,1:T(8,128)(2,1)S(1)} %get-tuple-element.110), channel_id=1, source_target_pairs={{496,0},{504,8},{0,16},{8,24},{16,32},{24,40},{32,48},{40,56},{48,... | collective-permute-start | bytes 786440 | tf_op jit(solution)/shard_map/ppermute | solution.py:17
  56.4 1.0 copy-start.1
  63.7 2.8 %copy-start.2 = (bf16[21,128,128]{2,1,0:T(8,128)(2,1)S(1)}, bf16[21,128,128]{2,1,0:T(8,128)(2,1)}, u32[]{:S(2)}) copy-start(bf16[21,128,128]{2,1,0:T(8,128)(2,1)} %copy-done.1) | copy-start | bytes 2064388 | tf_op jit(solution)/shard_map/while
  66.5 1.1 copy-start.1
  73.8 2.9 %copy-start.2 = (bf16[21,128,128]{2,1,0:T(8,128)(2,1)S(1)}, bf16[21,128,128]{2,1,0:T(8,128)(2,1)}, u32[]{:S(2)}) copy-start(bf16[21,128,128]{2,1,0:T(8,128)(2,1)} %copy-done.1) | copy-start | bytes 2064388 | tf_op jit(solution)/shard_map/while
  76.7 1.1 copy-start.1
  84.1 2.9 %copy-start.2 = (bf16[21,128,128]{2,1,0:T(8,128)(2,1)S(1)}, bf16[21,128,128]{2,1,0:T(8,128)(2,1)}, u32[]{:S(2)}) copy-start(bf16[21,128,128]{2,1,0:T(8,128)(2,1)} %copy-done.1) | copy-start | bytes 2064388 | tf_op jit(solution)/shard_map/while
  87.0 1.1 copy-start.1
  94.3 2.9 %copy-start.2 = (bf16[21,128,128]{2,1,0:T(8,128)(2,1)S(1)}, bf16[21,128,128]{2,1,0:T(8,128)(2,1)}, u32[]{:S(2)}) copy-start(bf16[21,128,128]{2,1,0:T(8,128)(2,1)} %copy-done.1) | copy-start | bytes 2064388 | tf_op jit(solution)/shard_map/while
  97.2 1.1 copy-start.1
  104.6 2.9 %copy-start.2 = (bf16[21,128,128]{2,1,0:T(8,128)(2,1)S(1)}, bf16[21,128,128]{2,1,0:T(8,128)(2,1)}, u32[]{:S(2)}) copy-start(bf16[21,128,128]{2,1,0:T(8,128)(2,1)} %copy-done.1) | copy-start | bytes 2064388 | tf_op jit(solution)/shard_map/while
  107.5 1.1 copy-start.1
  114.8 2.9 %copy-start.2 = (bf16[21,128,128]{2,1,0:T(8,128)(2,1)S(1)}, bf16[21,128,128]{2,1,0:T(8,128)(2,1)}, u32[]{:S(2)}) copy-start(bf16[21,128,128]{2,1,0:T(8,128)(2,1)} %copy-done.1) | copy-start | bytes 2064388 | tf_op jit(solution)/shard_map/while
  117.7 1.1 copy-start.1
  125.0 2.9 %copy-start.2 = (bf16[21,128,128]{2,1,0:T(8,128)(2,1)S(1)}, bf16[21,128,128]{2,1,0:T(8,128)(2,1)}, u32[]{:S(2)}) copy-start(bf16[21,128,128]{2,1,0:T(8,128)(2,1)} %copy-done.1) | copy-start | bytes 2064388 | tf_op jit(solution)/shard_map/while
  128.0 1.1 copy-start.1
  135.3 2.9 %copy-start.2 = (bf16[21,128,128]{2,1,0:T(8,128)(2,1)S(1)}, bf16[21,128,128]{2,1,0:T(8,128)(2,1)}, u32[]{:S(2)}) copy-start(bf16[21,128,128]{2,1,0:T(8,128)(2,1)} %copy-done.1) | copy-start | bytes 2064388 | tf_op jit(solution)/shard_map/while
  138.2 1.1 copy-start.1
  145.5 2.9 %copy-start.2 = (bf16[21,128,128]{2,1,0:T(8,128)(2,1)S(1)}, bf16[21,128,128]{2,1,0:T(8,128)(2,1)}, u32[]{:S(2)}) copy-start(bf16[21,128,128]{2,1,0:T(8,128)(2,1)} %copy-done.1) | copy-start | bytes 2064388 | tf_op jit(solution)/shard_map/while
  148.5 1.1 copy-start.1
  155.8 2.9 %copy-start.2 = (bf16[21,128,128]{2,1,0:T(8,128)(2,1)S(1)}, bf16[21,128,128]{2,1,0:T(8,128)(2,1)}, u32[]{:S(2)}) copy-start(bf16[21,128,128]{2,1,0:T(8,128)(2,1)} %copy-done.1) | copy-start | bytes 2064388 | tf_op jit(solution)/shard_map/while
  158.7 94.7 %copy-start.5 = (f32[6]{0:T(128)S(1)}, f32[6]{0:T(128)}, u32[]{:S(2)}) copy-start(f32[6]{0:T(128)} %param.21) | copy-start | bytes 76
  253.5 0.8 copy-start.3
Sparse Core Ops, SparseCore 0:
  160.8 91.7 all-reduce.1
where the time goes:
time: 265 us; the launch traced here: 261 us
  waiting for transfers between devices  80.3 us (30%)
  matrix products  75.1 us (28%)
  local copies, waits for them, and re-layouts  38.1 us (14%)
  starting transfers between devices  29.7 us (11%)
  blocking collectives  19.1 us (7%)
  between operations  14.3 us (5%)
  other arithmetic  4.04 us (2%)
    psum x1, waiting for transfers between devices, local(): totals, weight_total = lax.psum((numerator, weight_sum), 'band')  72.9 us
    dot_general x10, matrix products, place_block(): jnp.einsum('jid,jdq->jiq', matched, shifter, preferred_element_type=jnp.f...  32.1 us
    ppermute x8, starting transfers between devices, shifted(): return lax.ppermute(block, axis, route)  29.7 us
    dot_general x10, matrix products, place_block(): jnp.einsum('jb,jiq->biq', one_hot, placed, precision=HIGHEST_PRECISION)  27.2 us
    psum x1, blocking collectives, local(): totals, weight_total = lax.psum((numerator, weight_sum), 'band')  19.1 us
    dot_general x10, local copies, waits for them, and re-layouts, match_block(): jnp.einsum('jic,kdc->jkid', tiles_in, colmats, preferred_element_type=jnp...  18.3 us
    dynamic_slice x10, local copies, waits for them, and re-layouts, local(): lax.scan(accumulate, start_state, (slots.reshape(-1, 8, tile_rows, tile_w...  10.6 us
    dot_general x10, matrix products, match_block(): jnp.einsum('jic,kdc->jkid', tiles_in, colmats, preferred_element_type=jnp...  8.79 us
  transfers between devices with their start and end apart: 9, of which 4 were waited for; matrix products, arithmetic and copies ran while one was open for 3% of the time, Pallas kernels for 0%

commit v1 on v0

v1 whole, which is shorter than its diff:
```python
import jax
import jax.numpy as jnp
from jax import lax
from jax.experimental import pallas as pl
from jax.experimental.pallas import tpu as pltpu
from jax.sharding import PartitionSpec as P

PW = 256
BANDS = 6
REACH = 2
SPREAD = 2 * REACH + 1
F32 = jnp.float32
BF16 = jnp.bfloat16
MESH = pl.DeviceIdType.MESH
SIDES = [p for p in range(SPREAD) if p != REACH]


def kernel(
    n_ra,
    n_band,
    patch_s,
    off_s,
    vband_s,
    cidx_s,
    bw_s,
    ctab_s,
    tiles,
    wt,
    rowk,
    colk,
    out_ref,
    det_ref,
    kpad,
    rbase,
    cst,
    ps,
    mat,
    placed,
    a8,
    nbuf,
    own,
    recva,
    sumb,
    recvb,
    wbuf,
    wrecva,
    wsum,
    wrecvb,
    send_a,
    recv_a,
    send_b,
    recv_b,
    wsend_a,
    wrecv_a,
    wsend_b,
    wrecv_b,
):
    me_ra = lax.axis_index("ra")
    me_band = lax.axis_index("band")
    count, rows, width = tiles.shape
    basis, taps = rowk.shape
    half = taps // 2
    block = rows // n_band
    per_visit = count // vband_s.shape[0]

    def ra_at(distance):
        return lax.rem(me_ra + distance + n_ra, n_ra)

    def band_at(distance):
        return lax.rem(me_band + distance, n_band)

    barrier = pltpu.get_barrier_semaphore()
    for p in SIDES:
        pl.semaphore_signal(
            barrier, inc=1, device_id=(ra_at(p - REACH), me_band), device_id_type=MESH
        )
    for d in range(1, n_band):
        pl.semaphore_signal(
            barrier, inc=1, device_id=(me_ra, band_at(d)), device_id_type=MESH
        )

    lane = lax.broadcasted_iota(jnp.int32, (block, width), 1)
    sub = lax.broadcasted_iota(jnp.int32, (block, width), 0)
    kpad[...] = jnp.zeros_like(kpad)
    kpad[0:basis, 0:taps] = rowk[...].astype(F32)
    for k in range(basis):
        row = jnp.broadcast_to(kpad[k : k + 1, :], (block, width))
        rbase[k * block : (k + 1) * block, :] = pltpu.roll(
            row, width - half, 1, stride=1, stride_axis=0
        )
    kpad[0:basis, 0:taps] = colk[...].astype(F32)
    flip_r = lax.broadcasted_iota(jnp.int32, (width, width), 0)
    flip_c = lax.broadcasted_iota(jnp.int32, (width, width), 1)
    flip = jnp.where(flip_r + flip_c == taps - 1, 1.0, 0.0).astype(BF16)
    kpad[...] = jnp.dot(kpad[...].astype(BF16), flip, preferred_element_type=F32)

    def column_matrix(k, carry):
        row = jnp.broadcast_to(kpad[pl.ds(k, 1), :], (block, width))
        base = pltpu.roll(row, width - half, 1, stride=1, stride_axis=0)
        for c in range(0, width, 2 * block):
            parts = []
            for at in (c, c + block):
                part = base if at == 0 else pltpu.roll(base, at, 1)
                if at < half or at + block > width - half:
                    part = jnp.where(jnp.abs(lane - sub - at) <= half, part, 0.0)
                parts.append(part)
            cst[pl.ds(k * width + c, 2 * block), :] = jnp.concatenate(parts, axis=0).astype(BF16)
        return carry

    lax.fori_loop(0, basis, column_matrix, 0)

    spread_r = lax.broadcasted_iota(jnp.int32, (count, count * block), 0)
    spread_c = lax.broadcasted_iota(jnp.int32, (count, count * block), 1)
    spread = jnp.where(spread_c // block == spread_r, 1.0, 0.0).astype(BF16)
    w_lane = jnp.dot(
        jnp.broadcast_to(wt[...], (block, count)), spread, preferred_element_type=F32
    )
    lane8 = lax.broadcasted_iota(jnp.int32, (block, count * block), 1)
    sub8 = lax.broadcasted_iota(jnp.int32, (block, count * block), 0)
    bucket = jnp.zeros((block, count * block), jnp.int32)
    band = jnp.zeros((block, count * block), jnp.int32)
    for j in range(count):
        here = lane8 // block == j
        bucket = jnp.where(here, patch_s[j], bucket)
        band = jnp.where(here, vband_s[j // per_visit], band)
    bucket = bucket - me_ra + REACH
    bucket = jnp.where(bucket < 0, bucket + n_ra, bucket)
    bucket = jnp.where(bucket >= n_ra, bucket - n_ra, bucket)
    diag = lax.rem(lane8, block) == sub8
    for p in range(SPREAD):
        for b in range(0, BANDS, 2):
            parts = [
                jnp.where((bucket == p) & (band == b + h) & diag, w_lane, 0.0) for h in (0, 1)
            ]
            at = (p * BANDS + b) * block
            a8[at : at + 2 * block, :] = jnp.concatenate(parts, axis=0).astype(BF16)
    first = lax.rem(lane8, block) == 0
    aw = jnp.concatenate(
        [
            jnp.where((bucket == p) & (band == sub8) & first, w_lane, 0.0)
            for p in range(SPREAD)
        ]
        + [jnp.zeros((block, count * block), F32)],
        axis=0,
    ).astype(BF16)

    def cover(jp, carry):
        left, right = [], []
        for h in (0, 1):
            off = off_s[2 * jp + h]
            left.append(jnp.where(lane >= off, 1.0, 0.0))
            right.append(jnp.where(lane < off, 1.0, 0.0))
        at = pl.ds(pl.multiple_of(jp * 2 * block, 2 * block), 2 * block)
        placed[at, 0:width] = jnp.concatenate(left, axis=0).astype(BF16)
        placed[at, width : 2 * width] = jnp.concatenate(right, axis=0).astype(BF16)
        return carry

    lax.fori_loop(0, count // 2, cover, 0)
    sums = jnp.dot(aw, placed[...], preferred_element_type=F32)
    for p in range(SPREAD):
        wbuf[p] = sums[p * block : (p + 1) * block]

    def weight_a(i):
        p = SIDES[i]
        return pltpu.make_async_remote_copy(
            src_ref=wbuf.at[p],
            dst_ref=wrecva.at[i],
            send_sem=wsend_a.at[i],
            recv_sem=wrecv_a.at[i],
            device_id=(ra_at(p - REACH), me_band),
            device_id_type=MESH,
        )

    def weight_b(d):
        return pltpu.make_async_remote_copy(
            src_ref=wsum,
            dst_ref=wrecvb.at[d - 1],
            send_sem=wsend_b.at[d - 1],
            recv_sem=wrecv_b.at[d - 1],
            device_id=(me_ra, band_at(d)),
            device_id_type=MESH,
        )

    def part_a(i, s):
        p = SIDES[i]
        return pltpu.make_async_remote_copy(
            src_ref=nbuf.at[s, i],
            dst_ref=recva.at[s, i],
            send_sem=send_a.at[s, i],
            recv_sem=recv_a.at[s, i],
            device_id=(ra_at(p - REACH), me_band),
            device_id_type=MESH,
        )

    def part_b(s):
        return pltpu.make_async_remote_copy(
            src_ref=sumb.at[s],
            dst_ref=recvb.at[s],
            send_sem=send_b.at[s],
            recv_sem=recv_b.at[s],
            device_id=(me_ra, band_at(s + 1)),
            device_id_type=MESH,
        )

    def compute(s):
        r = lax.rem(me_band + 1 + s, n_band)
        taps_now = pltpu.roll(rbase[...], r * block, 1)[:, 0:rows].astype(BF16)

        def pair(jp, carry):
            t = jnp.concatenate([tiles[2 * jp], tiles[2 * jp + 1]], axis=1)
            x = jnp.dot(taps_now, t, preferred_element_type=F32)
            i0 = cidx_s[2 * jp]
            i1 = cidx_s[2 * jp + 1]
            at = pl.ds(pl.multiple_of(jp * 2 * block, 2 * block), 2 * block)
            for k in range(basis):
                x0 = x[k * block : (k + 1) * block, 0:width] * ctab_s[i0, k]
                x1 = x[k * block : (k + 1) * block, width : 2 * width] * ctab_s[i1, k]
                ps[at, k * width : (k + 1) * width] = jnp.concatenate([x0, x1], axis=0).astype(BF16)
            return carry

        lax.fori_loop(0, count // 2, pair, 0)
        mat[...] = jnp.dot(ps[...], cst[...], preferred_element_type=F32)

        def place(jp, carry):
            left, right = [], []
            for h in (0, 1):
                off = off_s[2 * jp + h]
                at = pl.ds(pl.multiple_of((2 * jp + h) * block, block), block)
                moved = pltpu.roll(mat[at, :], off, 1)
                left.append(jnp.where(lane >= off, moved, 0.0))
                right.append(jnp.where(lane < off, moved, 0.0))
            at = pl.ds(pl.multiple_of(jp * 2 * block, 2 * block), 2 * block)
            placed[at, 0:width] = jnp.concatenate(left, axis=0).astype(BF16)
            placed[at, width : 2 * width] = jnp.concatenate(right, axis=0).astype(BF16)
            return carry

        lax.fori_loop(0, count // 2, place, 0)
        n = jnp.dot(a8[...], placed[...], preferred_element_type=F32)
        size = BANDS * block
        for i, p in enumerate(SIDES):
            nbuf[s, i] = n[p * size : (p + 1) * size].astype(BF16)
        own[s] = n[REACH * size : (REACH + 1) * size]

    def patch_sum(s):
        total = own[s]
        for i in range(len(SIDES)):
            part_a(i, s).wait_recv()
            total = total + recva[s, i].astype(F32)
        return total

    pl.semaphore_wait(barrier, len(SIDES) + n_band - 1)
    for i in range(len(SIDES)):
        weight_a(i).start()

    def step(s, carry):
        compute(s)
        for i in range(len(SIDES)):
            part_a(i, s).start()

        @pl.when(s == 1)
        def _():
            total = wbuf[REACH]
            for i in range(len(SIDES)):
                weight_a(i).wait_recv()
                total = total + wrecva[i]
            wsum[...] = total
            for d in range(1, n_band):
                weight_b(d).start()

        @pl.when(s >= 2)
        def _():
            sumb[s - 2] = patch_sum(s - 2).astype(BF16)
            part_b(s - 2).start()

        return carry

    lax.fori_loop(0, n_band, step, 0)
    sumb[n_band - 2] = patch_sum(n_band - 2).astype(BF16)
    part_b(n_band - 2).start()
    total = patch_sum(n_band - 1)
    weights = wsum[...]
    for d in range(1, n_band):
        weight_b(d).wait_recv()
        weights = weights + wrecvb[d - 1]
    weights = jnp.maximum(weights, 1.0)
    for s in range(n_band - 1):
        part_b(s).wait_recv()
        total = total + recvb[s].astype(F32)
    detection = jnp.zeros((block, PW), F32)
    for b in range(BANDS):
        coadd = total[b * block : (b + 1) * block] / weights[b : b + 1]
        out_ref[b] = coadd
        detection = detection + bw_s[b] * coadd
    det_ref[...] = detection

    for i in range(len(SIDES)):
        weight_a(i).wait_send()
    for d in range(1, n_band):
        weight_b(d).wait_send()

    def drain(s, carry):
        for i in range(len(SIDES)):
            part_a(i, s).wait_send()

        @pl.when(s < n_band - 1)
        def _():
            part_b(s).wait_send()

        return carry

    lax.fori_loop(0, n_band, drain, 0)


def solution(mesh):
    n_ra, n_band = mesh.shape["ra"], mesh.shape["band"]

    def local(
        tiles,
        tile_patch,
        tile_offset,
        tile_weight,
        visit_band,
        coeff_index,
        coeff_table,
        row_kernels,
        column_kernels,
        band_weight,
    ):
        count, rows, width = tiles.shape
        basis = row_kernels.shape[0]
        block = rows // n_band
        size = BANDS * block
        sides = len(SIDES)
        smem = pl.BlockSpec(memory_space=pltpu.SMEM)
        vmem = pl.BlockSpec(memory_space=pltpu.VMEM)

        def body(*refs):
            kernel(n_ra, n_band, *refs)

        return pl.pallas_call(
            body,
            name="coadd",
            out_shape=(
                jax.ShapeDtypeStruct((BANDS, block, PW), F32),
                jax.ShapeDtypeStruct((block, PW), F32),
            ),
            in_specs=[smem] * 6 + [vmem] * 4,
            out_specs=(vmem, vmem),
            scratch_shapes=[
                pltpu.VMEM((24, width), F32),
                pltpu.VMEM((basis * block, width), F32),
                pltpu.VMEM((basis * width, width), BF16),
                pltpu.VMEM((count * block, basis * width), BF16),
                pltpu.VMEM((count * block, width), F32),
                pltpu.VMEM((count * block, PW), BF16),
                pltpu.VMEM((SPREAD * size, count * block), BF16),
                pltpu.VMEM((n_band, sides, size, PW), BF16),
                pltpu.VMEM((n_band, size, PW), F32),
                pltpu.VMEM((n_band, sides, size, PW), BF16),
                pltpu.VMEM((n_band, size, PW), BF16),
                pltpu.VMEM((n_band, size, PW), BF16),
                pltpu.VMEM((SPREAD, block, PW), F32),
                pltpu.VMEM((sides, block, PW), F32),
                pltpu.VMEM((block, PW), F32),
                pltpu.VMEM((n_band - 1, block, PW), F32),
                pltpu.SemaphoreType.DMA((n_band, sides)),
                pltpu.SemaphoreType.DMA((n_band, sides)),
                pltpu.SemaphoreType.DMA((n_band,)),
                pltpu.SemaphoreType.DMA((n_band,)),
                pltpu.SemaphoreType.DMA((sides,)),
                pltpu.SemaphoreType.DMA((sides,)),
                pltpu.SemaphoreType.DMA((n_band - 1,)),
                pltpu.SemaphoreType.DMA((n_band - 1,)),
            ],
            compiler_params=pltpu.CompilerParams(
                collective_id=0, has_side_effects=True, vmem_limit_bytes=48 * 1024 * 1024
            ),
        )(
            tile_patch,
            tile_offset,
            visit_band,
            coeff_index,
            band_weight,
            coeff_table,
            tiles,
            tile_weight.reshape(1, count),
            row_kernels,
            column_kernels,
        )

    return jax.shard_map(
        local,
        mesh=mesh,
        in_specs=(
            P(("ra", "band"), None, None),
            P(("ra", "band")),
            P(("ra", "band")),
            P(("ra", "band")),
            P(("ra", "band")),
            P(("ra", "band")),
            P(),
            P(),
            P(),
            P(),
        ),
        out_specs=(P(None, "band", "ra"), P("band", "ra")),
        check_vma=False,
    )
```

time: 265 us -> 60.5 us (0.23); the launches traced: 261 us -> 59.3 us
  waiting for transfers between devices: 80.3 us -> 0 us
  matrix products: 75.1 us -> 0 us
  Pallas kernels: 0 us -> 55.4 us
  local copies, waits for them, and re-layouts: 38.1 us -> 3.13 us
  starting transfers between devices: 29.7 us -> 0 us
  blocking collectives: 19.1 us -> 0 us
  between operations: 14.3 us -> 0.77 us
  other arithmetic: 4.04 us -> 0 us
    dot_general x55 -> x0, matrix products: 75.1 us -> none  [the longest x10 32.1 us: place_block(): jnp.einsum('jid,jdq->jiq', matched, shifter, preferred_element_type=jnp.f...]
    psum x1 -> x0, waiting for transfers between devices: 72.9 us -> none  [local(): totals, weight_total = lax.psum((numerator, weight_sum), 'band')]
    pallas_call x0 -> x1, Pallas kernels: none -> 55.4 us  [local(): pl.pallas_call(body, name='coadd', out_shape=(jax.ShapeDtypeStruct((BANDS...]
    ppermute x8 -> x0, starting transfers between devices: 29.7 us -> none  [shifted(): return lax.ppermute(block, axis, route)]
    psum x1 -> x0, blocking collectives: 19.1 us -> none  [local(): totals, weight_total = lax.psum((numerator, weight_sum), 'band')]
    dot_general x11 -> x0, local copies, waits for them, and re-layouts: 18.9 us -> none  [the longest x10 18.3 us: match_block(): jnp.einsum('jic,kdc->jkid', tiles_in, colmats, preferred_element_type=jnp...]
    dynamic_slice x10 -> x0, local copies, waits for them, and re-layouts: 10.6 us -> none  [local(): lax.scan(accumulate, start_state, (slots.reshape(-1, 8, tile_rows, tile_w...]
    ppermute x8 -> x0, waiting for transfers between devices: 7.46 us -> none  [shifted(): return lax.ppermute(block, axis, route)]
  transfers between devices with their start and end apart: 9 -> 0, of which waited for: 4 -> 0; matrix products, arithmetic and copies ran while one was open for 3% -> 0% of each run, Pallas kernels for 0% -> 0%
where the time goes in v1:
time: 60.5 us; the launch traced here: 59.3 us
  Pallas kernels  55.4 us (92%)
  local copies, waits for them, and re-layouts  3.13 us (5%)
  between operations  0.77 us (1%)
    pallas_call x1, Pallas kernels, local(): pl.pallas_call(body, name='coadd', out_shape=(jax.ShapeDtypeStruct((BANDS...  55.4 us
    unnamed x21, local copies, waits for them, and re-layouts  3.13 us

profile of v1, /device:TPU:24, one launch (start us, length us, event | category | flops | bytes accessed | tf_op | source)
XLA Modules:
  0.0 59.3 jit_solution(5191605575181375694)
XLA Ops:
  0.6 0.0 copy-start.1
  0.6 0.0 copy-start.2
  0.7 0.0 copy-start.3
  0.7 0.0 copy-start.4
  0.7 0.0 copy-start.5
  0.7 0.0 copy-start.6
  0.7 0.0 copy-start.7
  0.7 0.0 copy-start.8
  0.7 0.8 %copy.12.refs_5_ = f32[64,21]{1,0:T(8,128)S(1)} copy(f32[64,21]{0,1:T(8,128)} %param.16) | data formatting | bytes 10752 | tf_op args[6]
  1.6 0.0 copy-done.1
  1.6 0.0 copy-done.2
  1.6 0.0 copy-done.3
  1.6 0.0 copy-done.4
  1.6 0.0 copy-done.5
  1.6 0.0 copy-done.6
  1.6 0.0 copy-done.7
  1.6 0.0 copy-done.8
  1.6 0.0 copy-start
  1.6 1.0 %copy-done = bf16[32,64,128]{2,1,0:T(8,128)(2,1)S(1)} copy-done((bf16[32,64,128]{2,1,0:T(8,128)(2,1)S(1)}, bf16[32,64,128]{2,1,0:T(8,128)(2,1)}, u32[]{:S(2)}) %copy-start) | copy-done | bytes 524312
  2.7 55.4 %coadd.1 = (f32[6,8,256]{2,1,0:T(8,128)S(1)}, f32[8,256]{1,0:T(8,128)S(1)}) custom-call(s32[32]{0:T(128)S(1)} %copy-done.3, s32[32]{0:T(128)S(1)} %copy-done.4, s32[4]{0:T(128)S(1)} %copy-done.5, s32[32]{0:T(128)S(1)} %copy-done.6, f32[6]{0:T(128)S(1)} %copy-done.7, f32[64,21]{1,0:T(8,128)S(1)} %copy.12.refs_5_, bf16[32,64,128]{2,1,0:T(8,128)(2,1)S(1)} %copy-done, ...), custom_call_target="tpu_custom_call" | custom-call | tf_op jit(solution)/shard_map/coadd/pallas_call | solution.py:340
  58.1 0.6 %copy.15 = f32[6,8,256]{2,1,0:T(8,128)} copy(f32[6,8,256]{2,1,0:T(8,128)S(1)} %get-tuple-element.4) | data formatting | bytes 98304
  58.7 0.6 %copy.16 = f32[8,256]{1,0:T(8,128)} copy(f32[8,256]{1,0:T(8,128)S(1)} %get-tuple-element.5) | data formatting | bytes 16384
Async XLA Ops:
  0.6 0.9 %copy-start.1 = (bf16[21,21]{1,0:T(8,128)(2,1)S(1)}, bf16[21,21]{1,0:T(8,128)(2,1)}, u32[]{:S(2)}) copy-start(bf16[21,21]{1,0:T(8,128)(2,1)} %refs_8_.1) | copy-start | bytes 2650
  0.6 0.9 %copy-start.2 = (bf16[21,21]{1,0:T(8,128)(2,1)S(1)}, bf16[21,21]{1,0:T(8,128)(2,1)}, u32[]{:S(2)}) copy-start(bf16[21,21]{1,0:T(8,128)(2,1)} %refs_9_.1) | copy-start | bytes 2650
  0.7 0.9 %copy-start.3 = (s32[32]{0:T(128)S(1)}, s32[32]{0:T(128)}, u32[]{:S(2)}) copy-start(s32[32]{0:T(128)} %refs_0_.1) | copy-start | bytes 388
  0.7 0.9 %copy-start.4 = (s32[32]{0:T(128)S(1)}, s32[32]{0:T(128)}, u32[]{:S(2)}) copy-start(s32[32]{0:T(128)} %refs_1_.1) | copy-start | bytes 388
  0.7 0.9 %copy-start.5 = (s32[4]{0:T(128)S(1)}, s32[4]{0:T(128)}, u32[]{:S(2)}) copy-start(s32[4]{0:T(128)} %refs_2_.1) | copy-start | bytes 52
  0.7 0.9 %copy-start.6 = (s32[32]{0:T(128)S(1)}, s32[32]{0:T(128)}, u32[]{:S(2)}) copy-start(s32[32]{0:T(128)} %refs_3_.1) | copy-start | bytes 388
  0.7 0.9 %copy-start.7 = (f32[6]{0:T(128)S(1)}, f32[6]{0:T(128)}, u32[]{:S(2)}) copy-start(f32[6]{0:T(128)} %refs_4_.1) | copy-start | bytes 76
  0.7 0.9 %copy-start.8 = (bf16[32]{0:T(256)(128)(2,1)S(1)}, bf16[32]{0:T(256)(128)(2,1)}, u32[]{:S(2)}) copy-start(bf16[32]{0:T(256)(128)(2,1)} %param.13) | copy-start | bytes 196
  1.6 1.0 %copy-start = (bf16[32,64,128]{2,1,0:T(8,128)(2,1)S(1)}, bf16[32,64,128]{2,1,0:T(8,128)(2,1)}, u32[]{:S(2)}) copy-start(bf16[32,64,128]{2,1,0:T(8,128)(2,1)} %refs_6_.1) | copy-start | bytes 1572868

commit v2 on v1

--- a/solution.py
+++ b/solution.py
@@ -9,6 +9,7 @@
 BANDS = 6
 REACH = 2
 SPREAD = 2 * REACH + 1
+NB = 2
 F32 = jnp.float32
 BF16 = jnp.bfloat16
 MESH = pl.DeviceIdType.MESH
@@ -24,12 +25,14 @@
     cidx_s,
     bw_s,
     ctab_s,
-    tiles,
+    tiles_hbm,
     wt,
     rowk,
     colk,
     out_ref,
     det_ref,
+    tiles,
+    tile_sem,
     kpad,
     rbase,
     cst,
@@ -57,6 +60,8 @@
 ):
     me_ra = lax.axis_index("ra")
     me_band = lax.axis_index("band")
+    fetch = pltpu.make_async_copy(tiles_hbm, tiles, tile_sem)
+    fetch.start()
     count, rows, width = tiles.shape
     basis, taps = rowk.shape
     half = taps // 2
@@ -94,8 +99,8 @@
     flip = jnp.where(flip_r + flip_c == taps - 1, 1.0, 0.0).astype(BF16)
     kpad[...] = jnp.dot(kpad[...].astype(BF16), flip, preferred_element_type=F32)
 
-    def column_matrix(k, carry):
-        row = jnp.broadcast_to(kpad[pl.ds(k, 1), :], (block, width))
+    for k in range(basis):
+        row = jnp.broadcast_to(kpad[k : k + 1, :], (block, width))
         base = pltpu.roll(row, width - half, 1, stride=1, stride_axis=0)
         for c in range(0, width, 2 * block):
             parts = []
@@ -104,10 +109,7 @@
                 if at < half or at + block > width - half:
                     part = jnp.where(jnp.abs(lane - sub - at) <= half, part, 0.0)
                 parts.append(part)
-            cst[pl.ds(k * width + c, 2 * block), :] = jnp.concatenate(parts, axis=0).astype(BF16)
-        return carry
-
-    lax.fori_loop(0, basis, column_matrix, 0)
+            cst[k * width + c : k * width + c + 2 * block, :] = jnp.concatenate(parts, axis=0).astype(BF16)
 
     spread_r = lax.broadcasted_iota(jnp.int32, (count, count * block), 0)
     spread_c = lax.broadcasted_iota(jnp.int32, (count, count * block), 1)
@@ -144,18 +146,15 @@
         axis=0,
     ).astype(BF16)
 
-    def cover(jp, carry):
+    for jp in range(count // 2):
         left, right = [], []
         for h in (0, 1):
             off = off_s[2 * jp + h]
             left.append(jnp.where(lane >= off, 1.0, 0.0))
             right.append(jnp.where(lane < off, 1.0, 0.0))
-        at = pl.ds(pl.multiple_of(jp * 2 * block, 2 * block), 2 * block)
-        placed[at, 0:width] = jnp.concatenate(left, axis=0).astype(BF16)
-        placed[at, width : 2 * width] = jnp.concatenate(right, axis=0).astype(BF16)
-        return carry
-
-    lax.fori_loop(0, count // 2, cover, 0)
+        at = jp * 2 * block
+        placed[at : at + 2 * block, 0:width] = jnp.concatenate(left, axis=0).astype(BF16)
+        placed[at : at + 2 * block, width : 2 * width] = jnp.concatenate(right, axis=0).astype(BF16)
     sums = jnp.dot(aw, placed[...], preferred_element_type=F32)
     for p in range(SPREAD):
         wbuf[p] = sums[p * block : (p + 1) * block]
@@ -202,44 +201,49 @@
             device_id_type=MESH,
         )
 
-    def compute(s):
-        r = lax.rem(me_band + 1 + s, n_band)
-        taps_now = pltpu.roll(rbase[...], r * block, 1)[:, 0:rows].astype(BF16)
-
-        def pair(jp, carry):
-            t = jnp.concatenate([tiles[2 * jp], tiles[2 * jp + 1]], axis=1)
-            x = jnp.dot(taps_now, t, preferred_element_type=F32)
-            i0 = cidx_s[2 * jp]
-            i1 = cidx_s[2 * jp + 1]
-            at = pl.ds(pl.multiple_of(jp * 2 * block, 2 * block), 2 * block)
-            for k in range(basis):
-                x0 = x[k * block : (k + 1) * block, 0:width] * ctab_s[i0, k]
-                x1 = x[k * block : (k + 1) * block, width : 2 * width] * ctab_s[i1, k]
-                ps[at, k * width : (k + 1) * width] = jnp.concatenate([x0, x1], axis=0).astype(BF16)
-            return carry
-
-        lax.fori_loop(0, count // 2, pair, 0)
+    def compute(t):
+        parts = []
+        for h in range(NB):
+            r = lax.rem(me_band + 1 + NB * t + h, n_band)
+            parts.append(pltpu.roll(rbase[...], r * block, 1))
+        lhs = jnp.concatenate(
+            [
+                parts[h][k * block : (k + 1) * block, 0:rows]
+                for k in range(basis)
+                for h in range(NB)
+            ],
+            axis=0,
+        ).astype(BF16)
+        tall = NB * block
+        for jp in range(count // 2):
+            t2 = jnp.concatenate([tiles[2 * jp], tiles[2 * jp + 1]], axis=1)
+            x = jnp.dot(lhs, t2, preferred_element_type=F32)
+            for i in (0, 1):
+                j = 2 * jp + i
+                c = cidx_s[j]
+                for k in range(basis):
+                    y = x[k * tall : (k + 1) * tall, i * width : (i + 1) * width] * ctab_s[k, c]
+                    ps[j * tall : (j + 1) * tall, k * width : (k + 1) * width] = y.astype(BF16)
         mat[...] = jnp.dot(ps[...], cst[...], preferred_element_type=F32)
-
-        def place(jp, carry):
-            left, right = [], []
-            for h in (0, 1):
-                off = off_s[2 * jp + h]
-                at = pl.ds(pl.multiple_of((2 * jp + h) * block, block), block)
-                moved = pltpu.roll(mat[at, :], off, 1)
-                left.append(jnp.where(lane >= off, moved, 0.0))
-                right.append(jnp.where(lane < off, moved, 0.0))
-            at = pl.ds(pl.multiple_of(jp * 2 * block, 2 * block), 2 * block)
-            placed[at, 0:width] = jnp.concatenate(left, axis=0).astype(BF16)
-            placed[at, width : 2 * width] = jnp.concatenate(right, axis=0).astype(BF16)
-            return carry
-
-        lax.fori_loop(0, count // 2, place, 0)
-        n = jnp.dot(a8[...], placed[...], preferred_element_type=F32)
         size = BANDS * block
-        for i, p in enumerate(SIDES):
-            nbuf[s, i] = n[p * size : (p + 1) * size].astype(BF16)
-        own[s] = n[REACH * size : (REACH + 1) * size]
+        for h in range(NB):
+            for jp in range(count // 2):
+                left, right = [], []
+                for j in (2 * jp, 2 * jp + 1):
+                    off = off_s[j]
+                    at = j * tall + h * block
+                    moved = pltpu.roll(mat[at : at + block, :], off, 1)
+                    left.append(jnp.where(lane >= off, moved, 0.0))
+                    right.append(jnp.where(lane < off, moved, 0.0))
+                at = jp * 2 * block
+                placed[at : at + 2 * block, 0:width] = jnp.concatenate(left, axis=0).astype(BF16)
+                placed[at : at + 2 * block, width : 2 * width] = jnp.concatenate(
+                    right, axis=0
+                ).astype(BF16)
+            n = jnp.dot(a8[...], placed[...], preferred_element_type=F32)
+            for i, p in enumerate(SIDES):
+                nbuf[NB * t + h, i] = n[p * size : (p + 1) * size].astype(BF16)
+            own[NB * t + h] = n[REACH * size : (REACH + 1) * size]
 
     def patch_sum(s):
         total = own[s]
@@ -248,16 +252,18 @@
             total = total + recva[s, i].astype(F32)
         return total
 
+    fetch.wait()
     pl.semaphore_wait(barrier, len(SIDES) + n_band - 1)
     for i in range(len(SIDES)):
         weight_a(i).start()
 
-    def step(s, carry):
-        compute(s)
-        for i in range(len(SIDES)):
-            part_a(i, s).start()
-
-        @pl.when(s == 1)
+    def step(t, carry):
+        compute(t)
+        for h in range(NB):
+            for i in range(len(SIDES)):
+                part_a(i, NB * t + h).start()
+
+        @pl.when(t == 1)
         def _():
             total = wbuf[REACH]
             for i in range(len(SIDES)):
@@ -267,14 +273,19 @@
             for d in range(1, n_band):
                 weight_b(d).start()
 
-        @pl.when(s >= 2)
+        @pl.when(t >= 1)
         def _():
-            sumb[s - 2] = patch_sum(s - 2).astype(BF16)
-            part_b(s - 2).start()
+            for h in range(NB):
+                s = NB * t - NB + h
+                sumb[s] = patch_sum(s).astype(BF16)
+                part_b(s).start()
 
         return carry
 
-    lax.fori_loop(0, n_band, step, 0)
+    lax.fori_loop(0, n_band // NB, step, 0)
+    for s in range(n_band - NB, n_band - 2):
+        sumb[s] = patch_sum(s).astype(BF16)
+        part_b(s).start()
     sumb[n_band - 2] = patch_sum(n_band - 2).astype(BF16)
     part_b(n_band - 2).start()
     total = patch_sum(n_band - 1)
@@ -333,6 +344,7 @@
         sides = len(SIDES)
         smem = pl.BlockSpec(memory_space=pltpu.SMEM)
         vmem = pl.BlockSpec(memory_space=pltpu.VMEM)
+        hbm = pl.BlockSpec(memory_space=pltpu.HBM)
 
         def body(*refs):
             kernel(n_ra, n_band, *refs)
@@ -344,14 +356,16 @@
                 jax.ShapeDtypeStruct((BANDS, block, PW), F32),
                 jax.ShapeDtypeStruct((block, PW), F32),
             ),
-            in_specs=[smem] * 6 + [vmem] * 4,
+            in_specs=[smem] * 6 + [hbm] + [vmem] * 3,
             out_specs=(vmem, vmem),
             scratch_shapes=[
+                pltpu.VMEM((count, rows, width), BF16),
+                pltpu.SemaphoreType.DMA,
                 pltpu.VMEM((24, width), F32),
                 pltpu.VMEM((basis * block, width), F32),
                 pltpu.VMEM((basis * width, width), BF16),
-                pltpu.VMEM((count * block, basis * width), BF16),
-                pltpu.VMEM((count * block, width), F32),
+                pltpu.VMEM((NB * count * block, basis * width), BF16),
+                pltpu.VMEM((NB * count * block, width), F32),
                 pltpu.VMEM((count * block, PW), BF16),
                 pltpu.VMEM((SPREAD * size, count * block), BF16),
                 pltpu.VMEM((n_band, sides, size, PW), BF16),
@@ -381,7 +395,7 @@
             visit_band,
             coeff_index,
             band_weight,
-            coeff_table,
+            coeff_table.T,
             tiles,
             tile_weight.reshape(1, count),
             row_kernels,

time: 60.5 us -> 38.4 us (0.63); the launches traced: 59.3 us -> 38.1 us
  Pallas kernels: 55.4 us -> 32.4 us
  local copies, waits for them, and re-layouts: 3.13 us -> 5.04 us
    pallas_call x1, Pallas kernels: 55.4 us -> 32.4 us  [local(): pl.pallas_call(body, name='coadd', out_shape=(jax.ShapeDtypeStruct((BANDS...]
    unnamed x21 -> x22, local copies, waits for them, and re-layouts: 3.13 us -> 5.04 us
where the time goes in v2:
time: 38.4 us; the launch traced here: 38.1 us
  Pallas kernels  32.4 us (84%)
  local copies, waits for them, and re-layouts  5.04 us (13%)
  between operations  0.7 us (2%)
    pallas_call x1, Pallas kernels, local(): pl.pallas_call(body, name='coadd', out_shape=(jax.ShapeDtypeStruct((BANDS...  32.4 us
    unnamed x22, local copies, waits for them, and re-layouts  5.04 us

profile of v2, /device:TPU:24, one launch (start us, length us, event | category | flops | bytes accessed | tf_op | source)
XLA Modules:
  0.0 38.1 jit_solution(1397030590599467146)
XLA Ops:
  0.6 0.0 copy-start.7
  0.6 0.0 copy-start.8
  0.7 0.0 copy-start.9
  0.7 0.0 copy-start.4
  0.7 0.0 copy-start.5
  0.7 0.0 copy-start.6
  0.7 0.6 %copy-done.7 = s32[32]{0:T(128)S(1)} copy-done((s32[32]{0:T(128)S(1)}, s32[32]{0:T(128)}, u32[]{:S(2)}) %copy-start.7) | copy-done | bytes 152
  1.3 0.0 copy-done.8
  1.3 0.0 copy-done.9
  1.3 0.0 copy-done.4
  1.3 0.0 copy-done.5
  1.4 0.0 copy-done.6
  1.4 0.0 copy-start
  1.4 1.0 %copy-done = bf16[32,64,128]{2,1,0:T(8,128)(2,1)S(1)} copy-done((bf16[32,64,128]{2,1,0:T(8,128)(2,1)S(1)}, bf16[32,64,128]{2,1,0:T(8,128)(2,1)}, u32[]{:S(2)}) %copy-start) | copy-done | bytes 524312
  2.4 0.0 copy-start.1
  2.4 0.7 %copy-done.1 = f32[64,21]{0,1:T(8,128)S(1)} copy-done((f32[64,21]{0,1:T(8,128)S(1)}, f32[64,21]{0,1:T(8,128)}, u32[]{:S(2)}) %copy-start.1) | copy-done | bytes 5400
  3.1 0.0 copy-start.2
  3.1 0.7 %copy-done.2 = bf16[21,21]{1,0:T(8,128)(2,1)S(1)} copy-done((bf16[21,21]{1,0:T(8,128)(2,1)S(1)}, bf16[21,21]{1,0:T(8,128)(2,1)}, u32[]{:S(2)}) %copy-start.2) | copy-done | bytes 906
  3.8 0.0 copy-start.3
  3.8 0.7 %copy-done.3 = bf16[21,21]{1,0:T(8,128)(2,1)S(1)} copy-done((bf16[21,21]{1,0:T(8,128)(2,1)S(1)}, bf16[21,21]{1,0:T(8,128)(2,1)}, u32[]{:S(2)}) %copy-start.3) | copy-done | bytes 906
  4.5 32.4 %coadd.1 = (f32[6,8,256]{2,1,0:T(8,128)S(1)}, f32[8,256]{1,0:T(8,128)S(1)}) custom-call(s32[32]{0:T(128)S(1)} %copy-done.4, s32[32]{0:T(128)S(1)} %copy-done.5, s32[4]{0:T(128)S(1)} %copy-done.6, s32[32]{0:T(128)S(1)} %copy-done.7, f32[6]{0:T(128)S(1)} %copy-done.8, f32[21,64]{1,0:T(8,128)S(1)} %bitcast.2, bf16[32,64,128]{2,1,0:T(8,128)(2,1)S(1)} %copy-done, ...), custom_call_target="tpu_custom_call" | custom-call | tf_op jit(solution)/shard_map/coadd/pallas_call | solution.py:352
  36.9 0.6 %copy.14 = f32[6,8,256]{2,1,0:T(8,128)} copy(f32[6,8,256]{2,1,0:T(8,128)S(1)} %get-tuple-element.4) | data formatting | bytes 98304
  37.5 0.6 %copy.15 = f32[8,256]{1,0:T(8,128)} copy(f32[8,256]{1,0:T(8,128)S(1)} %get-tuple-element.5) | data formatting | bytes 16384
Async XLA Ops:
  0.6 0.7 %copy-start.7 = (s32[32]{0:T(128)S(1)}, s32[32]{0:T(128)}, u32[]{:S(2)}) copy-start(s32[32]{0:T(128)} %refs_3_.1) | copy-start | bytes 388
  0.6 0.7 %copy-start.8 = (f32[6]{0:T(128)S(1)}, f32[6]{0:T(128)}, u32[]{:S(2)}) copy-start(f32[6]{0:T(128)} %refs_4_.1) | copy-start | bytes 76
  0.7 0.7 %copy-start.9 = (bf16[32]{0:T(256)(128)(2,1)S(1)}, bf16[32]{0:T(256)(128)(2,1)}, u32[]{:S(2)}) copy-start(bf16[32]{0:T(256)(128)(2,1)} %param.13) | copy-start | bytes 196
  0.7 0.7 %copy-start.4 = (s32[32]{0:T(128)S(1)}, s32[32]{0:T(128)}, u32[]{:S(2)}) copy-start(s32[32]{0:T(128)} %refs_0_.1) | copy-start | bytes 388
  0.7 0.7 %copy-start.5 = (s32[32]{0:T(128)S(1)}, s32[32]{0:T(128)}, u32[]{:S(2)}) copy-start(s32[32]{0:T(128)} %refs_1_.1) | copy-start | bytes 388
  0.7 0.7 %copy-start.6 = (s32[4]{0:T(128)S(1)}, s32[4]{0:T(128)}, u32[]{:S(2)}) copy-start(s32[4]{0:T(128)} %refs_2_.1) | copy-start | bytes 52
  1.4 1.0 %copy-start = (bf16[32,64,128]{2,1,0:T(8,128)(2,1)S(1)}, bf16[32,64,128]{2,1,0:T(8,128)(2,1)}, u32[]{:S(2)}) copy-start(bf16[32,64,128]{2,1,0:T(8,128)(2,1)} %refs_6_.1) | copy-start | bytes 1572868
  2.4 0.7 %copy-start.1 = (f32[64,21]{0,1:T(8,128)S(1)}, f32[64,21]{0,1:T(8,128)}, u32[]{:S(2)}) copy-start(f32[64,21]{0,1:T(8,128)} %param.16) | copy-start | bytes 16132
  3.1 0.7 %copy-start.2 = (bf16[21,21]{1,0:T(8,128)(2,1)S(1)}, bf16[21,21]{1,0:T(8,128)(2,1)}, u32[]{:S(2)}) copy-start(bf16[21,21]{1,0:T(8,128)(2,1)} %refs_8_.1) | copy-start | bytes 2650
  3.8 0.7 %copy-start.3 = (bf16[21,21]{1,0:T(8,128)(2,1)S(1)}, bf16[21,21]{1,0:T(8,128)(2,1)}, u32[]{:S(2)}) copy-start(bf16[21,21]{1,0:T(8,128)(2,1)} %refs_9_.1) | copy-start | bytes 2650

commit v3 on v2

--- a/solution.py
+++ b/solution.py
@@ -10,6 +10,7 @@
 REACH = 2
 SPREAD = 2 * REACH + 1
 NB = 2
+VMEM_LIMIT = 60 * 1024 * 1024
 F32 = jnp.float32
 BF16 = jnp.bfloat16
 MESH = pl.DeviceIdType.MESH
@@ -19,20 +20,11 @@
 def kernel(
     n_ra,
     n_band,
-    patch_s,
-    off_s,
-    vband_s,
-    cidx_s,
-    bw_s,
-    ctab_s,
-    tiles_hbm,
-    wt,
-    rowk,
-    colk,
+    inputs,
     out_ref,
     det_ref,
-    tiles,
-    tile_sem,
+    held,
+    in_sem,
     kpad,
     rbase,
     cst,
@@ -60,8 +52,13 @@
 ):
     me_ra = lax.axis_index("ra")
     me_band = lax.axis_index("band")
-    fetch = pltpu.make_async_copy(tiles_hbm, tiles, tile_sem)
-    fetch.start()
+    fetches = [
+        pltpu.make_async_copy(src, dst, in_sem.at[i])
+        for i, (src, dst) in enumerate(zip(inputs, held))
+    ]
+    for fetch in fetches:
+        fetch.start()
+    patch_s, off_s, vband_s, cidx_s, bw_s, ctab_s, rowk, colk, wt, tiles = held
     count, rows, width = tiles.shape
     basis, taps = rowk.shape
     half = taps // 2
@@ -83,6 +80,9 @@
         pl.semaphore_signal(
             barrier, inc=1, device_id=(me_ra, band_at(d)), device_id_type=MESH
         )
+
+    for fetch in fetches[:-1]:
+        fetch.wait()
 
     lane = lax.broadcasted_iota(jnp.int32, (block, width), 1)
     sub = lax.broadcasted_iota(jnp.int32, (block, width), 0)
@@ -252,7 +252,7 @@
             total = total + recva[s, i].astype(F32)
         return total
 
-    fetch.wait()
+    fetches[-1].wait()
     pl.semaphore_wait(barrier, len(SIDES) + n_band - 1)
     for i in range(len(SIDES)):
         weight_a(i).start()
@@ -342,12 +342,27 @@
         block = rows // n_band
         size = BANDS * block
         sides = len(SIDES)
-        smem = pl.BlockSpec(memory_space=pltpu.SMEM)
         vmem = pl.BlockSpec(memory_space=pltpu.VMEM)
         hbm = pl.BlockSpec(memory_space=pltpu.HBM)
 
+        arrays = (
+            tile_patch,
+            tile_offset,
+            visit_band,
+            coeff_index,
+            band_weight,
+            coeff_table.T,
+            row_kernels,
+            column_kernels,
+            tile_weight.reshape(1, count),
+            tiles,
+        )
+        spaces = [pltpu.SMEM] * 6 + [pltpu.VMEM] * 4
+
         def body(*refs):
-            kernel(n_ra, n_band, *refs)
+            n = len(arrays)
+            held = refs[n + 2 : 2 * n + 2]
+            kernel(n_ra, n_band, refs[:n], *refs[n : n + 2], held, *refs[2 * n + 2 :])
 
         return pl.pallas_call(
             body,
@@ -356,11 +371,11 @@
                 jax.ShapeDtypeStruct((BANDS, block, PW), F32),
                 jax.ShapeDtypeStruct((block, PW), F32),
             ),
-            in_specs=[smem] * 6 + [hbm] + [vmem] * 3,
+            in_specs=[hbm] * len(arrays),
             out_specs=(vmem, vmem),
             scratch_shapes=[
-                pltpu.VMEM((count, rows, width), BF16),
-                pltpu.SemaphoreType.DMA,
+                *[space(a.shape, a.dtype) for space, a in zip(spaces, arrays)],
+                pltpu.SemaphoreType.DMA((len(arrays),)),
                 pltpu.VMEM((24, width), F32),
                 pltpu.VMEM((basis * block, width), F32),
                 pltpu.VMEM((basis * width, width), BF16),
@@ -387,20 +402,9 @@
                 pltpu.SemaphoreType.DMA((n_band - 1,)),
             ],
             compiler_params=pltpu.CompilerParams(
-                collective_id=0, has_side_effects=True, vmem_limit_bytes=48 * 1024 * 1024
+                collective_id=0, has_side_effects=True, vmem_limit_bytes=VMEM_LIMIT
             ),
-        )(
-            tile_patch,
-            tile_offset,
-            visit_band,
-            coeff_index,
-            band_weight,
-            coeff_table.T,
-            tiles,
-            tile_weight.reshape(1, count),
-            row_kernels,
-            column_kernels,
-        )
+        )(*arrays)
 
     return jax.shard_map(
         local,

time: 38.4 us -> 35.2 us (0.917)
  local copies, waits for them, and re-layouts: 5.04 us -> 2.03 us
    unnamed x22 -> x4, local copies, waits for them, and re-layouts: 5.04 us -> 2.03 us
where the time goes in v3:
time: 35.2 us; the launch traced here: 35 us
  Pallas kernels  32.3 us (92%)
  local copies, waits for them, and re-layouts  2.03 us (6%)
  between operations  0.65 us (2%)
    pallas_call x1, Pallas kernels, local(): pl.pallas_call(body, name='coadd', out_shape=(jax.ShapeDtypeStruct((BANDS...  32.3 us
    unnamed x4, local copies, waits for them, and re-layouts  2.03 us

profile of v3, /device:TPU:24, one launch (start us, length us, event | category | flops | bytes accessed | tf_op | source)
XLA Modules:
  0.0 35.0 jit_solution(3043112904751956990)
XLA Ops:
  0.6 32.3 %coadd.1 = (f32[6,8,256]{2,1,0:T(8,128)}, f32[8,256]{1,0:T(8,128)}) custom-call(s32[32]{0:T(128)} %refs_0_.1, s32[32]{0:T(128)} %refs_1_.1, s32[4]{0:T(128)} %refs_2_.1, s32[32]{0:T(128)} %refs_3_.1, f32[6]{0:T(128)} %refs_4_.1, f32[21,64]{1,0:T(8,128)} %bitcast.2, bf16[21,21]{1,0:T(8,128)(2,1)} %refs_6_.1, bf16[21,21]{1,0:T(8,128)(2,1)} %refs_7_.1, ...), custom_call_target="tpu_custom_call" | custom-call | tf_op jit(solution)/shard_map/coadd/pallas_call | solution.py:367
  32.9 0.0 copy-start
  32.9 1.4 %copy.14 = f32[6,8,256]{2,1,0:T(8,128)} copy(f32[6,8,256]{2,1,0:T(8,128)} %get-tuple-element.4) | data formatting | bytes 98304
  34.4 0.0 copy-done
  34.4 0.6 %copy.15 = f32[8,256]{1,0:T(8,128)} copy(f32[8,256]{1,0:T(8,128)S(1)} %copy-done) | data formatting | bytes 16384
Async XLA Ops:
  32.9 1.4 %copy-start = (f32[8,256]{1,0:T(8,128)S(1)}, f32[8,256]{1,0:T(8,128)}, u32[]{:S(2)}) copy-start(f32[8,256]{1,0:T(8,128)} %get-tuple-element.5) | copy-start | bytes 24580

commit v4 on v3

--- a/solution.py
+++ b/solution.py
@@ -10,6 +10,7 @@
 REACH = 2
 SPREAD = 2 * REACH + 1
 NB = 2
+LAG = 2
 VMEM_LIMIT = 60 * 1024 * 1024
 F32 = jnp.float32
 BF16 = jnp.bfloat16
@@ -253,17 +254,20 @@
         return total
 
     fetches[-1].wait()
-    pl.semaphore_wait(barrier, len(SIDES) + n_band - 1)
-    for i in range(len(SIDES)):
-        weight_a(i).start()
-
     def step(t, carry):
         compute(t)
+
+        @pl.when(t == 0)
+        def _():
+            pl.semaphore_wait(barrier, len(SIDES) + n_band - 1)
+            for i in range(len(SIDES)):
+                weight_a(i).start()
+
         for h in range(NB):
             for i in range(len(SIDES)):
                 part_a(i, NB * t + h).start()
 
-        @pl.when(t == 1)
+        @pl.when(t == 2)
         def _():
             total = wbuf[REACH]
             for i in range(len(SIDES)):
@@ -273,17 +277,17 @@
             for d in range(1, n_band):
                 weight_b(d).start()
 
-        @pl.when(t >= 1)
+        @pl.when(t >= LAG)
         def _():
             for h in range(NB):
-                s = NB * t - NB + h
+                s = NB * (t - LAG) + h
                 sumb[s] = patch_sum(s).astype(BF16)
                 part_b(s).start()
 
         return carry
 
     lax.fori_loop(0, n_band // NB, step, 0)
-    for s in range(n_band - NB, n_band - 2):
+    for s in range(n_band - LAG * NB, n_band - 2):
         sumb[s] = patch_sum(s).astype(BF16)
         part_b(s).start()
     sumb[n_band - 2] = patch_sum(n_band - 2).astype(BF16)
@@ -368,8 +372,8 @@
             body,
             name="coadd",
             out_shape=(
-                jax.ShapeDtypeStruct((BANDS, block, PW), F32),
-                jax.ShapeDtypeStruct((block, PW), F32),
+                pltpu.VMEM((BANDS, block, PW), F32),
+                pltpu.VMEM((block, PW), F32),
             ),
             in_specs=[hbm] * len(arrays),
             out_specs=(vmem, vmem),

time: 35.2 us -> 30.7 us (0.87)
  Pallas kernels: 32.3 us -> 28.7 us
  local copies, waits for them, and re-layouts: 2.03 us -> 1.22 us
    pallas_call x1, Pallas kernels: 32.3 us -> 28.7 us  [local(): pl.pallas_call(body, name='coadd', out_shape=(pltpu.VMEM((BANDS, block, P...]
    unnamed x4 -> x2, local copies, waits for them, and re-layouts: 2.03 us -> 1.22 us
where the time goes in v4:
time: 30.7 us; the launch traced here: 30.6 us
  Pallas kernels  28.7 us (93%)
  local copies, waits for them, and re-layouts  1.22 us (4%)
  between operations  0.64 us (2%)
    pallas_call x1, Pallas kernels, local(): pl.pallas_call(body, name='coadd', out_shape=(pltpu.VMEM((BANDS, block, P...  28.7 us
    unnamed x2, local copies, waits for them, and re-layouts  1.22 us

profile of v4, /device:TPU:24, one launch (start us, length us, event | category | flops | bytes accessed | tf_op | source)
XLA Modules:
  0.0 30.6 jit_solution(12002925627485109344)
XLA Ops:
  0.6 28.7 %coadd.1 = (f32[6,8,256]{2,1,0:T(8,128)S(1)}, f32[8,256]{1,0:T(8,128)S(1)}) custom-call(s32[32]{0:T(128)} %refs_0_.1, s32[32]{0:T(128)} %refs_1_.1, s32[4]{0:T(128)} %refs_2_.1, s32[32]{0:T(128)} %refs_3_.1, f32[6]{0:T(128)} %refs_4_.1, f32[21,64]{1,0:T(8,128)} %bitcast.2, bf16[21,21]{1,0:T(8,128)(2,1)} %refs_6_.1, bf16[21,21]{1,0:T(8,128)(2,1)} %refs_7_.1, ...), custom_call_target="tpu_custom_call" | custom-call | tf_op jit(solution)/shard_map/coadd/pallas_call | solution.py:371
  29.4 0.6 %copy.14 = f32[6,8,256]{2,1,0:T(8,128)} copy(f32[6,8,256]{2,1,0:T(8,128)S(1)} %get-tuple-element.2) | data formatting | bytes 98304
  30.0 0.6 %copy.15 = f32[8,256]{1,0:T(8,128)} copy(f32[8,256]{1,0:T(8,128)S(1)} %get-tuple-element.3) | data formatting | bytes 16384

commit v5 on v4

--- a/solution.py
+++ b/solution.py
@@ -10,12 +10,12 @@
 REACH = 2
 SPREAD = 2 * REACH + 1
 NB = 2
-LAG = 2
+LAG = 3
 VMEM_LIMIT = 60 * 1024 * 1024
 F32 = jnp.float32
 BF16 = jnp.bfloat16
 MESH = pl.DeviceIdType.MESH
-SIDES = [p for p in range(SPREAD) if p != REACH]
+SIDES = [0, 4, 1, 3]
 
 
 def kernel(
@@ -156,7 +156,7 @@
         at = jp * 2 * block
         placed[at : at + 2 * block, 0:width] = jnp.concatenate(left, axis=0).astype(BF16)
         placed[at : at + 2 * block, width : 2 * width] = jnp.concatenate(right, axis=0).astype(BF16)
-    sums = jnp.dot(aw, placed[...], preferred_element_type=F32)
+    sums = jnp.dot(aw, placed[:, 0:PW], preferred_element_type=F32)
     for p in range(SPREAD):
         wbuf[p] = sums[p * block : (p + 1) * block]
 
@@ -237,14 +237,16 @@
                     left.append(jnp.where(lane >= off, moved, 0.0))
                     right.append(jnp.where(lane < off, moved, 0.0))
                 at = jp * 2 * block
-                placed[at : at + 2 * block, 0:width] = jnp.concatenate(left, axis=0).astype(BF16)
-                placed[at : at + 2 * block, width : 2 * width] = jnp.concatenate(
-                    right, axis=0
-                ).astype(BF16)
-            n = jnp.dot(a8[...], placed[...], preferred_element_type=F32)
+                for part, q in ((left, h * PW), (right, h * PW + width)):
+                    placed[at : at + 2 * block, q : q + width] = jnp.concatenate(
+                        part, axis=0
+                    ).astype(BF16)
+        n = jnp.dot(a8[...], placed[...], preferred_element_type=F32)
+        for h in range(NB):
+            here = n[:, h * PW : (h + 1) * PW]
             for i, p in enumerate(SIDES):
-                nbuf[NB * t + h, i] = n[p * size : (p + 1) * size].astype(BF16)
-            own[NB * t + h] = n[REACH * size : (REACH + 1) * size]
+                nbuf[NB * t + h, i] = here[p * size : (p + 1) * size].astype(BF16)
+            own[NB * t + h] = here[REACH * size : (REACH + 1) * size]
 
     def patch_sum(s):
         total = own[s]
@@ -385,7 +387,7 @@
                 pltpu.VMEM((basis * width, width), BF16),
                 pltpu.VMEM((NB * count * block, basis * width), BF16),
                 pltpu.VMEM((NB * count * block, width), F32),
-                pltpu.VMEM((count * block, PW), BF16),
+                pltpu.VMEM((count * block, NB * PW), BF16),
                 pltpu.VMEM((SPREAD * size, count * block), BF16),
                 pltpu.VMEM((n_band, sides, size, PW), BF16),
                 pltpu.VMEM((n_band, size, PW), F32),

time: 30.7 us -> 30.7 us (level)
  no operation moved by 1% of the time
where the time goes in v5:
time: 30.7 us; the launch traced here: 30.5 us
  Pallas kernels  28.7 us (93%)
  local copies, waits for them, and re-layouts  1.22 us (4%)
  between operations  0.64 us (2%)
    pallas_call x1, Pallas kernels, local(): pl.pallas_call(body, name='coadd', out_shape=(pltpu.VMEM((BANDS, block, P...  28.7 us
    unnamed x2, local copies, waits for them, and re-layouts  1.22 us

profile of v5, /device:TPU:24, one launch (start us, length us, event | category | flops | bytes accessed | tf_op | source)
XLA Modules:
  0.0 30.5 jit_solution(17717698701115837390)
XLA Ops:
  0.6 28.7 %coadd.1 = (f32[6,8,256]{2,1,0:T(8,128)S(1)}, f32[8,256]{1,0:T(8,128)S(1)}) custom-call(s32[32]{0:T(128)} %refs_0_.1, s32[32]{0:T(128)} %refs_1_.1, s32[4]{0:T(128)} %refs_2_.1, s32[32]{0:T(128)} %refs_3_.1, f32[6]{0:T(128)} %refs_4_.1, f32[21,64]{1,0:T(8,128)} %bitcast.2, bf16[21,21]{1,0:T(8,128)(2,1)} %refs_6_.1, bf16[21,21]{1,0:T(8,128)(2,1)} %refs_7_.1, ...), custom_call_target="tpu_custom_call" | custom-call | tf_op jit(solution)/shard_map/coadd/pallas_call | solution.py:373
  29.3 0.6 %copy.14 = f32[6,8,256]{2,1,0:T(8,128)} copy(f32[6,8,256]{2,1,0:T(8,128)S(1)} %get-tuple-element.2) | data formatting | bytes 98304
  29.9 0.6 %copy.15 = f32[8,256]{1,0:T(8,128)} copy(f32[8,256]{1,0:T(8,128)S(1)} %get-tuple-element.3) | data formatting | bytes 16384
